TPU v7x, 256 devices: a whole 4x4x8 slice. The times are simulated.
256 devices in a mesh: slab: 32 (over y, z), mode: 8 (over x, core).
Axes of the slice: x: 4, y: 4, z: 8, core: 2. Of those that a mesh axis runs over, the one named last changes fastest.
Arguments:
- positions: float32 [3, 524288], P(None, ('slab', 'mode')), may hold values from 0 to 1, as said below
- charges: float32 [524288], P(('slab', 'mode')), may hold values from -0.03125 to 0.03125
- counts: int32 [32], replicated, may hold values from 3840 to 16384, as said below
- box: float32 [2], replicated, may hold values from 0.8 to 1.25
Outputs:
- forces: float32 [3, 524288], P(None, ('slab', 'mode'))
Inputs may be any that keep to these rules, and one draw needn't show every extreme that they name: positions[0] and positions[1] are fractional coordinates; positions[2, i] lies strictly between s 0.08 / 32 and (s + 1) 0.08 / 32 for s = i // 16384, and never falls with i within a slab. The live ions of a slab are its first counts[s] slots; some slab is full.
All inputs are finite; a program needn't handle non-finite values.
Results may differ from a plain program's by a relative error of at most 0.0003.
Values sent between devices are 32-bit elements; how exact they have to be, the bound alone decides.
A program may use at most 64 MiB of HBM per device.

v0:
```python
import math
import jax
import jax.numpy as jnp
from jax import lax
from jax.sharding import PartitionSpec as P

QDIM = 64
BLOCK = 512
MODES = 4096
two_pi = 2.0 * math.pi
slab_span = 0.08


def carried_in(value, axis, combine, identity, reverse):
    size, mine = (lax.axis_size(axis), lax.axis_index(axis))
    everything = jax.tree.map(lambda part: lax.all_gather(part, axis), value)
    start = jax.tree.map(
        lambda part, zero: jnp.broadcast_to(jnp.asarray(zero, part.dtype), part.shape),
        value,
        identity,
    )

    def lap(k, before):
        at = size - 1 - k if reverse else k
        reached = at > mine if reverse else at < mine
        new = combine(before, jax.tree.map(lambda part: part[at], everything))
        return jax.tree.map(lambda a, b: jnp.where(reached, a, b), new, before)

    return lax.fori_loop(0, size, lap, start)


def wave_table(first_mode, mode_count, box):
    mode_index = first_mode + jnp.arange(mode_count, dtype=jnp.int32)
    order_p = (mode_index // QDIM + 1).astype(jnp.float32)
    order_q = (mode_index % QDIM - QDIM // 2).astype(jnp.float32)
    wave_x = two_pi * order_p / box[0]
    wave_y = two_pi * order_q / box[1]
    wave_norm = jnp.sqrt(wave_x * wave_x + wave_y * wave_y)
    return (order_p, order_q, wave_x / wave_norm, wave_y / wave_norm, wave_norm)


def phase_terms(mode_info, coords, lower_edge, height):
    order_p, order_q, unit_x, unit_y, wave_norm = mode_info
    phase_angle = two_pi * (
        order_p[:, None] * coords[0][None, :] + order_q[:, None] * coords[1][None, :]
    )
    ion_depth = coords[2][None, :] - lower_edge
    e_low = jnp.exp(-wave_norm[:, None] * ion_depth)
    e_high = jnp.exp(-wave_norm[:, None] * (height - ion_depth))
    return (jnp.cos(phase_angle), jnp.sin(phase_angle), e_low, e_high)


def block_moments(mode_info, coords, weight, lower_edge, height):
    cosine, sine_part, e_low, e_high = phase_terms(mode_info, coords, lower_edge, height)
    upward = weight[None, :] * e_high
    downward = weight[None, :] * e_low
    row_stack = jnp.stack(
        [upward * cosine, upward * sine_part, downward * cosine, downward * sine_part]
    )
    mode_count = cosine.shape[0]
    return jnp.sum(row_stack.reshape(4, mode_count, cosine.shape[1] // BLOCK, BLOCK), axis=3)


def force_terms(mode_info, coords, weight, coefficients, lower_edge, height, box):
    order_p, order_q, unit_x, unit_y, wave_norm = mode_info
    cosine, sine_part, e_low, e_high = phase_terms(mode_info, coords, lower_edge, height)
    mode_count, ion_count = cosine.shape
    block_count = coefficients.shape[2]

    def spread(row_values):
        return jnp.broadcast_to(row_values[:, :, None], (mode_count, block_count, BLOCK)).reshape(
            mode_count, ion_count
        )

    below_c = e_low * spread(coefficients[0])
    below_s = e_low * spread(coefficients[1])
    above_c = e_high * spread(coefficients[2])
    above_s = e_high * spread(coefficients[3])
    in_plane = sine_part * (below_c + above_c) - cosine * (below_s + above_s)
    normal = cosine * (below_c - above_c) + sine_part * (below_s - above_s)
    scale = 2.0 * two_pi / (box[0] * box[1]) * weight
    return (
        jnp.stack(
            [
                jnp.sum(unit_x[:, None] * in_plane, axis=0),
                jnp.sum(unit_y[:, None] * in_plane, axis=0),
                jnp.sum(normal, axis=0),
            ]
        )
        * scale[None, :]
    )


def group_blocks(ion_total):
    block_count = ion_total // BLOCK
    chosen = 1
    for factor in range(1, 5):
        if block_count % factor == 0:
            chosen = factor
    return chosen


def sweep_moments(mode_info, coords, weight, lower_edge, height):
    ion_total = coords.shape[1]
    per_group = group_blocks(ion_total)
    group_width = per_group * BLOCK
    group_count = ion_total // group_width
    coord_groups = coords.reshape(3, group_count, group_width).transpose(1, 0, 2)
    weight_groups = weight.reshape(group_count, group_width)

    def advance(carried, group_item):
        return (carried, block_moments(mode_info, group_item[0], group_item[1], lower_edge, height))

    _, pieces = lax.scan(advance, jnp.int32(0), (coord_groups, weight_groups))
    mode_count = pieces.shape[2]
    return pieces.transpose(1, 2, 0, 3).reshape(4, mode_count, group_count * per_group)


def sweep_forces(mode_info, coords, weight, coefficients, lower_edge, height, box):
    ion_total = coords.shape[1]
    per_group = group_blocks(ion_total)
    group_width = per_group * BLOCK
    group_count = ion_total // group_width
    mode_count = coefficients.shape[1]
    coord_groups = coords.reshape(3, group_count, group_width).transpose(1, 0, 2)
    weight_groups = weight.reshape(group_count, group_width)
    coeff_groups = coefficients.reshape(4, mode_count, group_count, per_group).transpose(2, 0, 1, 3)

    def advance(carried, group_item):
        return (
            carried,
            force_terms(
                mode_info, group_item[0], group_item[1], group_item[2], lower_edge, height, box
            ),
        )

    _, pieces = lax.scan(advance, jnp.int32(0), (coord_groups, weight_groups, coeff_groups))
    return pieces.transpose(1, 0, 2).reshape(3, ion_total)


def carry_coefficients(moments, wave_norm, height):
    mode_count = moments.shape[1]
    block_count = moments.shape[2]
    block_ids = jnp.arange(block_count, dtype=jnp.int32)
    lower_tri = (block_ids[:, None] < block_ids[None, :]).astype(jnp.float32)
    upper_tri = (block_ids[:, None] > block_ids[None, :]).astype(jnp.float32)
    prefix_up = jnp.dot(
        moments[0:2].reshape(2 * mode_count, block_count),
        lower_tri,
        precision=lax.Precision.HIGHEST,
    ).reshape(2, mode_count, block_count)
    suffix_down = jnp.dot(
        moments[2:4].reshape(2 * mode_count, block_count),
        upper_tri,
        precision=lax.Precision.HIGHEST,
    ).reshape(2, mode_count, block_count)
    totals = jnp.sum(moments, axis=2)
    decay_step = jnp.exp(-wave_norm * height)

    def compose(earlier, later):
        return (earlier[0] * later[0], earlier[1] * later[0][None, :] + later[1])

    identity = (jnp.ones_like(decay_step), jnp.zeros((2, mode_count), jnp.float32))
    _, carry_up = carried_in((decay_step, totals[0:2]), "slab", compose, identity, False)
    _, carry_down = carried_in((decay_step, totals[2:4]), "slab", compose, identity, True)
    boost_step = jnp.exp(wave_norm * height)[None, :, None]
    return jnp.concatenate(
        [
            carry_up[:, :, None] + boost_step * prefix_up,
            carry_down[:, :, None] + boost_step * suffix_down,
        ],
        axis=0,
    )


def shards(positions, charges, counts, box):
    slab_count = lax.axis_size("slab")
    mode_parts = lax.axis_size("mode")
    slab_rank = lax.axis_index("slab")
    mode_rank = lax.axis_index("mode")
    modes_dev = MODES // mode_parts
    height = slab_span / slab_count
    lower_edge = slab_rank.astype(jnp.float32) * height
    live_count = jnp.sum(jnp.where(jnp.arange(slab_count, dtype=jnp.int32) == slab_rank, counts, 0))
    coords, charge = (
        lax.all_gather(positions, "mode", axis=1, tiled=True),
        lax.all_gather(charges, "mode", axis=0, tiled=True),
    )
    live_mask = jnp.arange(coords.shape[1], dtype=jnp.int32) < live_count
    weight = jnp.where(live_mask, charge, jnp.float32(0.0))
    mode_info = wave_table(mode_rank * modes_dev, modes_dev, box)
    moments = sweep_moments(mode_info, coords, weight, lower_edge, height)
    coefficients = carry_coefficients(moments, mode_info[4], height)
    partial_force = sweep_forces(mode_info, coords, weight, coefficients, lower_edge, height, box)
    return lax.psum_scatter(partial_force, "mode", scatter_dimension=1, tiled=True)


def solution(mesh):
    return jax.shard_map(
        shards,
        mesh=mesh,
        in_specs=(P(None, ("slab", "mode")), P(("slab", "mode")), P(), P()),
        out_specs=P(None, ("slab", "mode")),
        check_vma=False,
    )
```

profile of v0, /device:TPU:1, one launch (start us, length us, event | category | flops | bytes accessed | tf_op | source)
XLA Modules:
  0.0 587.2 jit_solution(16965568512662683384)
XLA Ops:
  13.1 16.0 %all_gather.26 = f32[16384]{0:T(1024)S(1)} all-gather(f32[2048]{0:T(1024)} %param.13), channel_id=1, replica_groups=mesh['slab'=32,'mode'=8] {'mode'}, dimensions={0}, use_global_device_ids=true | all-gather | bytes 73728 | tf_op jit(solution)/shard_map/all_gather | solution.py:187
  29.8 13.1 %all_gather.24 = f32[3,16384]{1,0:T(4,128)S(1)} all-gather(f32[3,2048]{1,0:T(4,128)} %param.12), channel_id=1, replica_groups=mesh['slab'=32,'mode'=8] {'mode'}, dimensions={1}, use_global_device_ids=true | all-gather | bytes 221184 | tf_op jit(solution)/shard_map/all_gather | solution.py:186
  42.9 161.3 %while.60 = (s32[]{:T(128)}, f32[8,4,512,4]{2,3,1,0:T(4,128)S(1)}, f32[8,2048]{1,0:T(8,128)S(1)}, f32[8,3,2048]{2,1,0:T(4,128)S(1)}, f32[]{:T(128)}, /*index=5*/...) while((s32[]{:T(128)}, f32[8,4,512,4]{2,3,1,0:T(4,128)S(1)}, ...), condition=%wide.region_3.4_spmd.clone.clone, body=%wide.region_1.3_spmd.clone.clone.sunk | while | flops 29384708 | bytes 33853620 | solution.py:114
  44.3 17.2 %fusion.91 = (f32[1,512,4,512]{3,1,2,0:T(8,128)S(1)}, f32[1,512,4,512]{3,1,2,0:T(8,128)S(1)}, f32[1,512,4,512]{3,1,2,0:T(8,128)S(1)}, f32[1,512,4,512]{3,1,2,0:T(8,128)S(1)}) fusion(f32[4,512]{1,0:T(4,128)S(1)} %mul.1380, f32[512]{0:T(512)S(1)} %get-tuple-element.909, f32[4,512]{1,0:T(4,128)S(1)} %mul.1381, f32[512]{0:T(512)S(1)} %get-tuple-element.911, ...), kind=kLoop, calls=%fused_computation.21.clone.1 | loop fusion | flops 12582912 | bytes 16824320 | tf_op jit(solution)/shard_map/while/body/eval_jaxpr/mul | solution.py:58
  61.5 1.4 maximum_reduce_fusion.2
  64.5 17.2 %fusion.91 = (f32[1,512,4,512]{3,1,2,0:T(8,128)S(1)}, f32[1,512,4,512]{3,1,2,0:T(8,128)S(1)}, f32[1,512,4,512]{3,1,2,0:T(8,128)S(1)}, f32[1,512,4,512]{3,1,2,0:T(8,128)S(1)}) fusion(f32[4,512]{1,0:T(4,128)S(1)} %mul.1380, f32[512]{0:T(512)S(1)} %get-tuple-element.909, f32[4,512]{1,0:T(4,128)S(1)} %mul.1381, f32[512]{0:T(512)S(1)} %get-tuple-element.911, ...), kind=kLoop, calls=%fused_computation.21.clone.1 | loop fusion | flops 12582912 | bytes 16824320 | tf_op jit(solution)/shard_map/while/body/eval_jaxpr/mul | solution.py:58
  81.7 1.4 maximum_reduce_fusion.2
  84.7 17.2 %fusion.91 = (f32[1,512,4,512]{3,1,2,0:T(8,128)S(1)}, f32[1,512,4,512]{3,1,2,0:T(8,128)S(1)}, f32[1,512,4,512]{3,1,2,0:T(8,128)S(1)}, f32[1,512,4,512]{3,1,2,0:T(8,128)S(1)}) fusion(f32[4,512]{1,0:T(4,128)S(1)} %mul.1380, f32[512]{0:T(512)S(1)} %get-tuple-element.909, f32[4,512]{1,0:T(4,128)S(1)} %mul.1381, f32[512]{0:T(512)S(1)} %get-tuple-element.911, ...), kind=kLoop, calls=%fused_computation.21.clone.1 | loop fusion | flops 12582912 | bytes 16824320 | tf_op jit(solution)/shard_map/while/body/eval_jaxpr/mul | solution.py:58
  104.8 17.2 %fusion.91 = (f32[1,512,4,512]{3,1,2,0:T(8,128)S(1)}, f32[1,512,4,512]{3,1,2,0:T(8,128)S(1)}, f32[1,512,4,512]{3,1,2,0:T(8,128)S(1)}, f32[1,512,4,512]{3,1,2,0:T(8,128)S(1)}) fusion(f32[4,512]{1,0:T(4,128)S(1)} %mul.1380, f32[512]{0:T(512)S(1)} %get-tuple-element.909, f32[4,512]{1,0:T(4,128)S(1)} %mul.1381, f32[512]{0:T(512)S(1)} %get-tuple-element.911, ...), kind=kLoop, calls=%fused_computation.21.clone.1 | loop fusion | flops 12582912 | bytes 16824320 | tf_op jit(solution)/shard_map/while/body/eval_jaxpr/mul | solution.py:58
  125.0 17.2 %fusion.91 = (f32[1,512,4,512]{3,1,2,0:T(8,128)S(1)}, f32[1,512,4,512]{3,1,2,0:T(8,128)S(1)}, f32[1,512,4,512]{3,1,2,0:T(8,128)S(1)}, f32[1,512,4,512]{3,1,2,0:T(8,128)S(1)}) fusion(f32[4,512]{1,0:T(4,128)S(1)} %mul.1380, f32[512]{0:T(512)S(1)} %get-tuple-element.909, f32[4,512]{1,0:T(4,128)S(1)} %mul.1381, f32[512]{0:T(512)S(1)} %get-tuple-element.911, ...), kind=kLoop, calls=%fused_computation.21.clone.1 | loop fusion | flops 12582912 | bytes 16824320 | tf_op jit(solution)/shard_map/while/body/eval_jaxpr/mul | solution.py:58
  145.2 17.2 %fusion.91 = (f32[1,512,4,512]{3,1,2,0:T(8,128)S(1)}, f32[1,512,4,512]{3,1,2,0:T(8,128)S(1)}, f32[1,512,4,512]{3,1,2,0:T(8,128)S(1)}, f32[1,512,4,512]{3,1,2,0:T(8,128)S(1)}) fusion(f32[4,512]{1,0:T(4,128)S(1)} %mul.1380, f32[512]{0:T(512)S(1)} %get-tuple-element.909, f32[4,512]{1,0:T(4,128)S(1)} %mul.1381, f32[512]{0:T(512)S(1)} %get-tuple-element.911, ...), kind=kLoop, calls=%fused_computation.21.clone.1 | loop fusion | flops 12582912 | bytes 16824320 | tf_op jit(solution)/shard_map/while/body/eval_jaxpr/mul | solution.py:58
  165.3 17.2 %fusion.91 = (f32[1,512,4,512]{3,1,2,0:T(8,128)S(1)}, f32[1,512,4,512]{3,1,2,0:T(8,128)S(1)}, f32[1,512,4,512]{3,1,2,0:T(8,128)S(1)}, f32[1,512,4,512]{3,1,2,0:T(8,128)S(1)}) fusion(f32[4,512]{1,0:T(4,128)S(1)} %mul.1380, f32[512]{0:T(512)S(1)} %get-tuple-element.909, f32[4,512]{1,0:T(4,128)S(1)} %mul.1381, f32[512]{0:T(512)S(1)} %get-tuple-element.911, ...), kind=kLoop, calls=%fused_computation.21.clone.1 | loop fusion | flops 12582912 | bytes 16824320 | tf_op jit(solution)/shard_map/while/body/eval_jaxpr/mul | solution.py:58
  182.5 1.4 maximum_reduce_fusion.2
  185.5 17.2 %fusion.91 = (f32[1,512,4,512]{3,1,2,0:T(8,128)S(1)}, f32[1,512,4,512]{3,1,2,0:T(8,128)S(1)}, f32[1,512,4,512]{3,1,2,0:T(8,128)S(1)}, f32[1,512,4,512]{3,1,2,0:T(8,128)S(1)}) fusion(f32[4,512]{1,0:T(4,128)S(1)} %mul.1380, f32[512]{0:T(512)S(1)} %get-tuple-element.909, f32[4,512]{1,0:T(4,128)S(1)} %mul.1381, f32[512]{0:T(512)S(1)} %get-tuple-element.911, ...), kind=kLoop, calls=%fused_computation.21.clone.1 | loop fusion | flops 12582912 | bytes 16824320 | tf_op jit(solution)/shard_map/while/body/eval_jaxpr/mul | solution.py:58
  202.7 1.4 maximum_reduce_fusion.2
  204.2 35.3 %all-gather.3 = f32[32,2,512]{2,1,0:T(2,128)S(1)} all-gather(f32[1,2,512]{2,1,0:T(2,128)S(1)} %get-tuple-element.719), channel_id=2, replica_groups=mesh['slab'=32,'mode'=8] {'slab'}, dimensions={0}, use_global_device_ids=true | all-gather | bytes 135168 | tf_op jit(solution)/shard_map/all_gather | solution.py:16
  239.6 36.0 %all-gather.2 = f32[32,1,512]{2,1,0:T(1,128)S(1)} all-gather(f32[1,1,512]{2,1,0:T(1,128)S(1)} %exponential_bitcast_fusion), channel_id=1, replica_groups=mesh['slab'=32,'mode'=8] {'slab'}, dimensions={0}, use_global_device_ids=true | all-gather | bytes 67584 | tf_op jit(solution)/shard_map/all_gather | solution.py:16
  275.5 1.9 while.58
  277.5 31.4 %all-gather.4 = f32[32,2,512]{2,1,0:T(2,128)S(1)} all-gather(f32[1,2,512]{2,1,0:T(2,128)S(1)} %get-tuple-element.720), channel_id=3, replica_groups=mesh['slab'=32,'mode'=8] {'slab'}, dimensions={0}, use_global_device_ids=true | all-gather | bytes 135168 | tf_op jit(solution)/shard_map/all_gather | solution.py:16
  308.9 2.3 while.59
  311.8 178.5 %while.61 = (s32[]{:T(128)}, f32[8,3,2048]{2,1,0:T(4,128)S(1)}, f32[8,3,2048]{2,1,0:T(4,128)S(1)}, f32[]{:T(128)}, f32[8,4,512,4]{2,3,1,0:T(4,128)S(1)}, /*index...) while((s32[]{:T(128)}, f32[8,3,2048]{2,1,0:T(4,128)S(1)}, ...), condition=%wide.region_13.14_spmd.clone.clone, body=%wide.region_9.13_spmd.clone.clone.sunk | while | flops 26279428 | bytes 422137 | solution.py:137
  314.6 19.4 %multiply_reduce_fusion.3 = (f32[4,512]{1,0:T(4,128)S(1)}, f32[4,512]{1,0:T(4,128)S(1)}, f32[4,512]{1,0:T(4,128)S(1)}) fusion(f32[512,4]{0,1:T(4,128)S(1)} %get-tuple-element.927, f32[512,4]{0,1:T(4,128)S(1)} %get-tuple-element.928, f32[512,4]{0,1:T(4,128)S(1)} %get-tuple-element.929, f32[4,512]{1,0:T(4,128)S(1)} %broadcast_subtract_fusion.5, ...), kind=kLoop, calls=%fused_computation.59.clone.1 | loop fusion | flops 26208256 | bytes 100352 | tf_op jit(solution)/shard_map/while/body/eval_jaxpr/reduce_sum | solution.py:85
  336.9 19.4 %multiply_reduce_fusion.3 = (f32[4,512]{1,0:T(4,128)S(1)}, f32[4,512]{1,0:T(4,128)S(1)}, f32[4,512]{1,0:T(4,128)S(1)}) fusion(f32[512,4]{0,1:T(4,128)S(1)} %get-tuple-element.927, f32[512,4]{0,1:T(4,128)S(1)} %get-tuple-element.928, f32[512,4]{0,1:T(4,128)S(1)} %get-tuple-element.929, f32[4,512]{1,0:T(4,128)S(1)} %broadcast_subtract_fusion.5, ...), kind=kLoop, calls=%fused_computation.59.clone.1 | loop fusion | flops 26208256 | bytes 100352 | tf_op jit(solution)/shard_map/while/body/eval_jaxpr/reduce_sum | solution.py:85
  359.2 19.4 %multiply_reduce_fusion.3 = (f32[4,512]{1,0:T(4,128)S(1)}, f32[4,512]{1,0:T(4,128)S(1)}, f32[4,512]{1,0:T(4,128)S(1)}) fusion(f32[512,4]{0,1:T(4,128)S(1)} %get-tuple-element.927, f32[512,4]{0,1:T(4,128)S(1)} %get-tuple-element.928, f32[512,4]{0,1:T(4,128)S(1)} %get-tuple-element.929, f32[4,512]{1,0:T(4,128)S(1)} %broadcast_subtract_fusion.5, ...), kind=kLoop, calls=%fused_computation.59.clone.1 | loop fusion | flops 26208256 | bytes 100352 | tf_op jit(solution)/shard_map/while/body/eval_jaxpr/reduce_sum | solution.py:85
  381.5 19.4 %multiply_reduce_fusion.3 = (f32[4,512]{1,0:T(4,128)S(1)}, f32[4,512]{1,0:T(4,128)S(1)}, f32[4,512]{1,0:T(4,128)S(1)}) fusion(f32[512,4]{0,1:T(4,128)S(1)} %get-tuple-element.927, f32[512,4]{0,1:T(4,128)S(1)} %get-tuple-element.928, f32[512,4]{0,1:T(4,128)S(1)} %get-tuple-element.929, f32[4,512]{1,0:T(4,128)S(1)} %broadcast_subtract_fusion.5, ...), kind=kLoop, calls=%fused_computation.59.clone.1 | loop fusion | flops 26208256 | bytes 100352 | tf_op jit(solution)/shard_map/while/body/eval_jaxpr/reduce_sum | solution.py:85
  403.8 19.4 %multiply_reduce_fusion.3 = (f32[4,512]{1,0:T(4,128)S(1)}, f32[4,512]{1,0:T(4,128)S(1)}, f32[4,512]{1,0:T(4,128)S(1)}) fusion(f32[512,4]{0,1:T(4,128)S(1)} %get-tuple-element.927, f32[512,4]{0,1:T(4,128)S(1)} %get-tuple-element.928, f32[512,4]{0,1:T(4,128)S(1)} %get-tuple-element.929, f32[4,512]{1,0:T(4,128)S(1)} %broadcast_subtract_fusion.5, ...), kind=kLoop, calls=%fused_computation.59.clone.1 | loop fusion | flops 26208256 | bytes 100352 | tf_op jit(solution)/shard_map/while/body/eval_jaxpr/reduce_sum | solution.py:85
  426.2 19.4 %multiply_reduce_fusion.3 = (f32[4,512]{1,0:T(4,128)S(1)}, f32[4,512]{1,0:T(4,128)S(1)}, f32[4,512]{1,0:T(4,128)S(1)}) fusion(f32[512,4]{0,1:T(4,128)S(1)} %get-tuple-element.927, f32[512,4]{0,1:T(4,128)S(1)} %get-tuple-element.928, f32[512,4]{0,1:T(4,128)S(1)} %get-tuple-element.929, f32[4,512]{1,0:T(4,128)S(1)} %broadcast_subtract_fusion.5, ...), kind=kLoop, calls=%fused_computation.59.clone.1 | loop fusion | flops 26208256 | bytes 100352 | tf_op jit(solution)/shard_map/while/body/eval_jaxpr/reduce_sum | solution.py:85
  448.5 19.4 %multiply_reduce_fusion.3 = (f32[4,512]{1,0:T(4,128)S(1)}, f32[4,512]{1,0:T(4,128)S(1)}, f32[4,512]{1,0:T(4,128)S(1)}) fusion(f32[512,4]{0,1:T(4,128)S(1)} %get-tuple-element.927, f32[512,4]{0,1:T(4,128)S(1)} %get-tuple-element.928, f32[512,4]{0,1:T(4,128)S(1)} %get-tuple-element.929, f32[4,512]{1,0:T(4,128)S(1)} %broadcast_subtract_fusion.5, ...), kind=kLoop, calls=%fused_computation.59.clone.1 | loop fusion | flops 26208256 | bytes 100352 | tf_op jit(solution)/shard_map/while/body/eval_jaxpr/reduce_sum | solution.py:85
  470.8 19.4 %multiply_reduce_fusion.3 = (f32[4,512]{1,0:T(4,128)S(1)}, f32[4,512]{1,0:T(4,128)S(1)}, f32[4,512]{1,0:T(4,128)S(1)}) fusion(f32[512,4]{0,1:T(4,128)S(1)} %get-tuple-element.927, f32[512,4]{0,1:T(4,128)S(1)} %get-tuple-element.928, f32[512,4]{0,1:T(4,128)S(1)} %get-tuple-element.929, f32[4,512]{1,0:T(4,128)S(1)} %broadcast_subtract_fusion.5, ...), kind=kLoop, calls=%fused_computation.59.clone.1 | loop fusion | flops 26208256 | bytes 100352 | tf_op jit(solution)/shard_map/while/body/eval_jaxpr/reduce_sum | solution.py:85
  490.3 5.1 copy.33
  495.4 82.8 %reduce-scatter.4.cloned.1.call-done = f32[2048,3]{1,0:T(8,128)} async-done(((f32[16384,3]{1,0:T(8,128)}), f32[2048,3]{1,0:T(8,128)}) %reduce-scatter.4.cloned.1.call-update) | async-done | bytes 24592
  578.2 2.2 copy.34
  (349 shorter events, 48.6 us)
Async XLA Ops:
  6.5 571.7 %reduce-scatter.4.cloned.1.call-start = ((), (), s32[]{:S(2)}) async-start(), calls=%async_computation.1 | async-start | bytes 9437184
Sparse Core Ops, SparseCore 0:
  495.6 82.6 reduce-scatter.3
where the time goes:
time: 588 us; the launch traced here: 587 us
  other arithmetic  343 us (58%)
  blocking collectives  132 us (22%)
  waiting for transfers between devices  82.8 us (14%)
  between operations  14.9 us (3%)
  local copies, waits for them, and re-layouts  11.1 us (2%)
    reduce_sum x8, other arithmetic, force_terms(): jnp.sum(unit_x[:, None] * in_plane, axis=0)  155 us
    mul x8, other arithmetic, block_moments(): upward * cosine  137 us
    all_gather x3, blocking collectives, carried_in(): everything = jax.tree.map(lambda part: lax.all_gather(part, axis), value)  103 us
    unnamed x2, waiting for transfers between devices  82.8 us
    neg x16, other arithmetic, phase_terms(): e_high = jnp.exp(-wave_norm[:, None] * (height - ion_depth))  20.6 us
    all_gather x1, blocking collectives, shards(): lax.all_gather(charges, 'mode', axis=0, tiled=True)  16 us
    all_gather x1, blocking collectives, shards(): lax.all_gather(positions, 'mode', axis=1, tiled=True)  13.1 us
  transfers between devices with their start and end apart: 1, of which 1 were waited for; matrix products, arithmetic and copies ran while one was open for 0% of the time, Pallas kernels for 0%

commit v1 on v0

--- a/solution.py
+++ b/solution.py
@@ -9,6 +9,15 @@
 MODES = 4096
 two_pi = 2.0 * math.pi
 slab_span = 0.08
+
+
+def treat_values(in_array):
+    in_order = []
+    for _ in range(lax.axis_size("mode")):
+        in_order.append(in_array)
+    return jnp.concatenate(
+        lax.all_to_all(jnp.stack(in_order), "mode", split_axis=0, concat_axis=0), 0
+    )
 
 
 def carried_in(value, axis, combine, identity, reverse):
@@ -182,10 +191,7 @@
     height = slab_span / slab_count
     lower_edge = slab_rank.astype(jnp.float32) * height
     live_count = jnp.sum(jnp.where(jnp.arange(slab_count, dtype=jnp.int32) == slab_rank, counts, 0))
-    coords, charge = (
-        lax.all_gather(positions, "mode", axis=1, tiled=True),
-        lax.all_gather(charges, "mode", axis=0, tiled=True),
-    )
+    coords, charge = (lax.all_gather(positions, "mode", axis=1, tiled=True), treat_values(charges))
     live_mask = jnp.arange(coords.shape[1], dtype=jnp.int32) < live_count
     weight = jnp.where(live_mask, charge, jnp.float32(0.0))
     mode_info = wave_table(mode_rank * modes_dev, modes_dev, box)

time: 588 us -> 580 us (0.986)
  waiting for transfers between devices: 82.8 us -> 71.1 us
  starting transfers between devices: 0.01 us -> 6.45 us
    all_gather x1 -> x0, blocking collectives: 16 us -> none  [shards(): lax.all_gather(charges, 'mode', axis=0, tiled=True)]
    all_gather x1, blocking collectives: 13.1 us -> 26.2 us  [shards(): lax.all_gather(positions, 'mode', axis=1, tiled=True)]
    unnamed x2, waiting for transfers between devices: 82.8 us -> 71.1 us
    all_to_all x0 -> x1, starting transfers between devices: none -> 6.45 us  [treat_values(): lax.all_to_all(jnp.stack(in_order), 'mode', split_axis=0, concat_axis=0)]
  transfers between devices with their start and end apart: 1 -> 2, of which waited for: 1 -> 1; matrix products, arithmetic and copies ran while one was open for 0% -> 1% of each run, Pallas kernels for 0% -> 0%
where the time goes in v1:
time: 580 us
  other arithmetic  342 us (59%)
  blocking collectives  129 us (22%)
  waiting for transfers between devices  71.1 us (12%)
  between operations  14.8 us (3%)
  local copies, waits for them, and re-layouts  12.4 us (2%)
  starting transfers between devices  6.45 us (1%)
    reduce_sum x8, other arithmetic, force_terms(): jnp.sum(unit_x[:, None] * in_plane, axis=0)  155 us
    mul x8, other arithmetic, block_moments(): upward * cosine  137 us
    all_gather x3, blocking collectives, carried_in(): everything = jax.tree.map(lambda part: lax.all_gather(part, axis), value)  103 us
    unnamed x2, waiting for transfers between devices  71.1 us
    all_gather x1, blocking collectives, shards(): lax.all_gather(positions, 'mode', axis=1, tiled=True)  26.2 us
    neg x16, other arithmetic, phase_terms(): e_high = jnp.exp(-wave_norm[:, None] * (height - ion_depth))  20.2 us
  transfers between devices with their start and end apart: 2, of which 1 were waited for; matrix products, arithmetic and copies ran while one was open for 1% of the time, Pallas kernels for 0%

profile of v1, /device:TPU:1, one launch (start us, length us, event | category | flops | bytes accessed | tf_op | source)
XLA Modules:
  0.0 579.7 jit_solution(10222998891475443336)
XLA Ops:
  7.9 6.5 %all-to-all-start = ((f32[8,1,2048]{2,1,0:T(1,128)}), f32[8,1,2048]{2,1,0:T(1,128)S(1)}, u32[]{:S(2)}, u32[]{:S(2)}) async-start(f32[8,1,2048]{2,1,0:T(1,128)} %stack.12), calls=%async_computation | async-start | bytes 131072 | tf_op jit(solution)/shard_map/all_to_all | solution.py:19
  20.8 39.2 %all-gather.2 = f32[32,1,512]{2,1,0:T(1,128)S(1)} all-gather(f32[1,1,512]{2,1,0:T(1,128)S(1)} %exponential_bitcast_fusion), channel_id=1, replica_groups=mesh['slab'=32,'mode'=8] {'slab'}, dimensions={0}, use_global_device_ids=true | all-gather | bytes 67584 | tf_op jit(solution)/shard_map/all_gather | solution.py:25
  60.0 26.2 %all_gather.21 = f32[3,16384]{1,0:T(4,128)S(1)} all-gather(f32[3,2048]{1,0:T(4,128)} %param.12), channel_id=1, replica_groups=mesh['slab'=32,'mode'=8] {'mode'}, dimensions={1}, use_global_device_ids=true | all-gather | bytes 221184 | tf_op jit(solution)/shard_map/all_gather | solution.py:194
  86.9 161.1 %while.60 = (s32[]{:T(128)}, f32[8,4,512,4]{2,3,1,0:T(4,128)S(1)}, f32[8,2048]{1,0:T(8,128)S(1)}, f32[8,3,2048]{2,1,0:T(4,128)S(1)}, f32[]{:T(128)}, /*index=5*/...) while((s32[]{:T(128)}, f32[8,4,512,4]{2,3,1,0:T(4,128)S(1)}, ...), condition=%wide.region_3.4_spmd.clone.clone, body=%wide.region_1.3_spmd.clone.clone.sunk | while | flops 29384708 | bytes 33853620 | solution.py:123
  88.4 17.2 %fusion.90 = (f32[1,512,4,512]{3,1,2,0:T(8,128)S(1)}, f32[1,512,4,512]{3,1,2,0:T(8,128)S(1)}, f32[1,512,4,512]{3,1,2,0:T(8,128)S(1)}, f32[1,512,4,512]{3,1,2,0:T(8,128)S(1)}) fusion(f32[4,512]{1,0:T(4,128)S(1)} %mul.1380, f32[512]{0:T(512)S(1)} %get-tuple-element.909, f32[4,512]{1,0:T(4,128)S(1)} %mul.1381, f32[512]{0:T(512)S(1)} %get-tuple-element.911, ...), kind=kLoop, calls=%fused_computation.21.clone.1 | loop fusion | flops 12582912 | bytes 16824320 | tf_op jit(solution)/shard_map/while/body/eval_jaxpr/mul | solution.py:67
  105.6 1.4 maximum_reduce_fusion.2
  108.5 17.2 %fusion.90 = (f32[1,512,4,512]{3,1,2,0:T(8,128)S(1)}, f32[1,512,4,512]{3,1,2,0:T(8,128)S(1)}, f32[1,512,4,512]{3,1,2,0:T(8,128)S(1)}, f32[1,512,4,512]{3,1,2,0:T(8,128)S(1)}) fusion(f32[4,512]{1,0:T(4,128)S(1)} %mul.1380, f32[512]{0:T(512)S(1)} %get-tuple-element.909, f32[4,512]{1,0:T(4,128)S(1)} %mul.1381, f32[512]{0:T(512)S(1)} %get-tuple-element.911, ...), kind=kLoop, calls=%fused_computation.21.clone.1 | loop fusion | flops 12582912 | bytes 16824320 | tf_op jit(solution)/shard_map/while/body/eval_jaxpr/mul | solution.py:67
  128.7 17.2 %fusion.90 = (f32[1,512,4,512]{3,1,2,0:T(8,128)S(1)}, f32[1,512,4,512]{3,1,2,0:T(8,128)S(1)}, f32[1,512,4,512]{3,1,2,0:T(8,128)S(1)}, f32[1,512,4,512]{3,1,2,0:T(8,128)S(1)}) fusion(f32[4,512]{1,0:T(4,128)S(1)} %mul.1380, f32[512]{0:T(512)S(1)} %get-tuple-element.909, f32[4,512]{1,0:T(4,128)S(1)} %mul.1381, f32[512]{0:T(512)S(1)} %get-tuple-element.911, ...), kind=kLoop, calls=%fused_computation.21.clone.1 | loop fusion | flops 12582912 | bytes 16824320 | tf_op jit(solution)/shard_map/while/body/eval_jaxpr/mul | solution.py:67
  145.8 1.4 maximum_reduce_fusion.2
  148.8 17.2 %fusion.90 = (f32[1,512,4,512]{3,1,2,0:T(8,128)S(1)}, f32[1,512,4,512]{3,1,2,0:T(8,128)S(1)}, f32[1,512,4,512]{3,1,2,0:T(8,128)S(1)}, f32[1,512,4,512]{3,1,2,0:T(8,128)S(1)}) fusion(f32[4,512]{1,0:T(4,128)S(1)} %mul.1380, f32[512]{0:T(512)S(1)} %get-tuple-element.909, f32[4,512]{1,0:T(4,128)S(1)} %mul.1381, f32[512]{0:T(512)S(1)} %get-tuple-element.911, ...), kind=kLoop, calls=%fused_computation.21.clone.1 | loop fusion | flops 12582912 | bytes 16824320 | tf_op jit(solution)/shard_map/while/body/eval_jaxpr/mul | solution.py:67
  168.9 17.2 %fusion.90 = (f32[1,512,4,512]{3,1,2,0:T(8,128)S(1)}, f32[1,512,4,512]{3,1,2,0:T(8,128)S(1)}, f32[1,512,4,512]{3,1,2,0:T(8,128)S(1)}, f32[1,512,4,512]{3,1,2,0:T(8,128)S(1)}) fusion(f32[4,512]{1,0:T(4,128)S(1)} %mul.1380, f32[512]{0:T(512)S(1)} %get-tuple-element.909, f32[4,512]{1,0:T(4,128)S(1)} %mul.1381, f32[512]{0:T(512)S(1)} %get-tuple-element.911, ...), kind=kLoop, calls=%fused_computation.21.clone.1 | loop fusion | flops 12582912 | bytes 16824320 | tf_op jit(solution)/shard_map/while/body/eval_jaxpr/mul | solution.py:67
  189.1 17.2 %fusion.90 = (f32[1,512,4,512]{3,1,2,0:T(8,128)S(1)}, f32[1,512,4,512]{3,1,2,0:T(8,128)S(1)}, f32[1,512,4,512]{3,1,2,0:T(8,128)S(1)}, f32[1,512,4,512]{3,1,2,0:T(8,128)S(1)}) fusion(f32[4,512]{1,0:T(4,128)S(1)} %mul.1380, f32[512]{0:T(512)S(1)} %get-tuple-element.909, f32[4,512]{1,0:T(4,128)S(1)} %mul.1381, f32[512]{0:T(512)S(1)} %get-tuple-element.911, ...), kind=kLoop, calls=%fused_computation.21.clone.1 | loop fusion | flops 12582912 | bytes 16824320 | tf_op jit(solution)/shard_map/while/body/eval_jaxpr/mul | solution.py:67
  206.3 1.4 maximum_reduce_fusion.2
  209.2 17.2 %fusion.90 = (f32[1,512,4,512]{3,1,2,0:T(8,128)S(1)}, f32[1,512,4,512]{3,1,2,0:T(8,128)S(1)}, f32[1,512,4,512]{3,1,2,0:T(8,128)S(1)}, f32[1,512,4,512]{3,1,2,0:T(8,128)S(1)}) fusion(f32[4,512]{1,0:T(4,128)S(1)} %mul.1380, f32[512]{0:T(512)S(1)} %get-tuple-element.909, f32[4,512]{1,0:T(4,128)S(1)} %mul.1381, f32[512]{0:T(512)S(1)} %get-tuple-element.911, ...), kind=kLoop, calls=%fused_computation.21.clone.1 | loop fusion | flops 12582912 | bytes 16824320 | tf_op jit(solution)/shard_map/while/body/eval_jaxpr/mul | solution.py:67
  226.4 1.4 maximum_reduce_fusion.2
  229.3 17.2 %fusion.90 = (f32[1,512,4,512]{3,1,2,0:T(8,128)S(1)}, f32[1,512,4,512]{3,1,2,0:T(8,128)S(1)}, f32[1,512,4,512]{3,1,2,0:T(8,128)S(1)}, f32[1,512,4,512]{3,1,2,0:T(8,128)S(1)}) fusion(f32[4,512]{1,0:T(4,128)S(1)} %mul.1380, f32[512]{0:T(512)S(1)} %get-tuple-element.909, f32[4,512]{1,0:T(4,128)S(1)} %mul.1381, f32[512]{0:T(512)S(1)} %get-tuple-element.911, ...), kind=kLoop, calls=%fused_computation.21.clone.1 | loop fusion | flops 12582912 | bytes 16824320 | tf_op jit(solution)/shard_map/while/body/eval_jaxpr/mul | solution.py:67
  248.1 32.2 %all-gather.3 = f32[32,2,512]{2,1,0:T(2,128)S(1)} all-gather(f32[1,2,512]{2,1,0:T(2,128)S(1)} %get-tuple-element.719), channel_id=2, replica_groups=mesh['slab'=32,'mode'=8] {'slab'}, dimensions={0}, use_global_device_ids=true | all-gather | bytes 135168 | tf_op jit(solution)/shard_map/all_gather | solution.py:25
  280.3 1.8 while.58
  282.3 31.2 %all-gather.4 = f32[32,2,512]{2,1,0:T(2,128)S(1)} all-gather(f32[1,2,512]{2,1,0:T(2,128)S(1)} %get-tuple-element.720), channel_id=3, replica_groups=mesh['slab'=32,'mode'=8] {'slab'}, dimensions={0}, use_global_device_ids=true | all-gather | bytes 135168 | tf_op jit(solution)/shard_map/all_gather | solution.py:25
  313.5 2.3 while.59
  316.4 178.1 %while.61 = (s32[]{:T(128)}, f32[8,3,2048]{2,1,0:T(4,128)S(1)}, f32[8,3,2048]{2,1,0:T(4,128)S(1)}, f32[]{:T(128)}, f32[8,4,512,4]{2,3,1,0:T(4,128)S(1)}, /*index...) while((s32[]{:T(128)}, f32[8,3,2048]{2,1,0:T(4,128)S(1)}, ...), condition=%wide.region_13.14_spmd.clone.clone, body=%wide.region_9.13_spmd.clone.clone.sunk | while | flops 26279428 | bytes 422137 | solution.py:146
  319.1 19.4 %multiply_reduce_fusion.3 = (f32[4,512]{1,0:T(4,128)S(1)}, f32[4,512]{1,0:T(4,128)S(1)}, f32[4,512]{1,0:T(4,128)S(1)}) fusion(f32[512,4]{0,1:T(4,128)S(1)} %get-tuple-element.927, f32[512,4]{0,1:T(4,128)S(1)} %get-tuple-element.928, f32[512,4]{0,1:T(4,128)S(1)} %get-tuple-element.929, f32[4,512]{1,0:T(4,128)S(1)} %broadcast_subtract_fusion.5, ...), kind=kLoop, calls=%fused_computation.59.clone.1 | loop fusion | flops 26208256 | bytes 100352 | tf_op jit(solution)/shard_map/while/body/eval_jaxpr/reduce_sum | solution.py:94
  341.3 19.4 %multiply_reduce_fusion.3 = (f32[4,512]{1,0:T(4,128)S(1)}, f32[4,512]{1,0:T(4,128)S(1)}, f32[4,512]{1,0:T(4,128)S(1)}) fusion(f32[512,4]{0,1:T(4,128)S(1)} %get-tuple-element.927, f32[512,4]{0,1:T(4,128)S(1)} %get-tuple-element.928, f32[512,4]{0,1:T(4,128)S(1)} %get-tuple-element.929, f32[4,512]{1,0:T(4,128)S(1)} %broadcast_subtract_fusion.5, ...), kind=kLoop, calls=%fused_computation.59.clone.1 | loop fusion | flops 26208256 | bytes 100352 | tf_op jit(solution)/shard_map/while/body/eval_jaxpr/reduce_sum | solution.py:94
  363.6 19.4 %multiply_reduce_fusion.3 = (f32[4,512]{1,0:T(4,128)S(1)}, f32[4,512]{1,0:T(4,128)S(1)}, f32[4,512]{1,0:T(4,128)S(1)}) fusion(f32[512,4]{0,1:T(4,128)S(1)} %get-tuple-element.927, f32[512,4]{0,1:T(4,128)S(1)} %get-tuple-element.928, f32[512,4]{0,1:T(4,128)S(1)} %get-tuple-element.929, f32[4,512]{1,0:T(4,128)S(1)} %broadcast_subtract_fusion.5, ...), kind=kLoop, calls=%fused_computation.59.clone.1 | loop fusion | flops 26208256 | bytes 100352 | tf_op jit(solution)/shard_map/while/body/eval_jaxpr/reduce_sum | solution.py:94
  385.9 19.4 %multiply_reduce_fusion.3 = (f32[4,512]{1,0:T(4,128)S(1)}, f32[4,512]{1,0:T(4,128)S(1)}, f32[4,512]{1,0:T(4,128)S(1)}) fusion(f32[512,4]{0,1:T(4,128)S(1)} %get-tuple-element.927, f32[512,4]{0,1:T(4,128)S(1)} %get-tuple-element.928, f32[512,4]{0,1:T(4,128)S(1)} %get-tuple-element.929, f32[4,512]{1,0:T(4,128)S(1)} %broadcast_subtract_fusion.5, ...), kind=kLoop, calls=%fused_computation.59.clone.1 | loop fusion | flops 26208256 | bytes 100352 | tf_op jit(solution)/shard_map/while/body/eval_jaxpr/reduce_sum | solution.py:94
  408.1 19.4 %multiply_reduce_fusion.3 = (f32[4,512]{1,0:T(4,128)S(1)}, f32[4,512]{1,0:T(4,128)S(1)}, f32[4,512]{1,0:T(4,128)S(1)}) fusion(f32[512,4]{0,1:T(4,128)S(1)} %get-tuple-element.927, f32[512,4]{0,1:T(4,128)S(1)} %get-tuple-element.928, f32[512,4]{0,1:T(4,128)S(1)} %get-tuple-element.929, f32[4,512]{1,0:T(4,128)S(1)} %broadcast_subtract_fusion.5, ...), kind=kLoop, calls=%fused_computation.59.clone.1 | loop fusion | flops 26208256 | bytes 100352 | tf_op jit(solution)/shard_map/while/body/eval_jaxpr/reduce_sum | solution.py:94
  430.4 19.4 %multiply_reduce_fusion.3 = (f32[4,512]{1,0:T(4,128)S(1)}, f32[4,512]{1,0:T(4,128)S(1)}, f32[4,512]{1,0:T(4,128)S(1)}) fusion(f32[512,4]{0,1:T(4,128)S(1)} %get-tuple-element.927, f32[512,4]{0,1:T(4,128)S(1)} %get-tuple-element.928, f32[512,4]{0,1:T(4,128)S(1)} %get-tuple-element.929, f32[4,512]{1,0:T(4,128)S(1)} %broadcast_subtract_fusion.5, ...), kind=kLoop, calls=%fused_computation.59.clone.1 | loop fusion | flops 26208256 | bytes 100352 | tf_op jit(solution)/shard_map/while/body/eval_jaxpr/reduce_sum | solution.py:94
  452.7 19.4 %multiply_reduce_fusion.3 = (f32[4,512]{1,0:T(4,128)S(1)}, f32[4,512]{1,0:T(4,128)S(1)}, f32[4,512]{1,0:T(4,128)S(1)}) fusion(f32[512,4]{0,1:T(4,128)S(1)} %get-tuple-element.927, f32[512,4]{0,1:T(4,128)S(1)} %get-tuple-element.928, f32[512,4]{0,1:T(4,128)S(1)} %get-tuple-element.929, f32[4,512]{1,0:T(4,128)S(1)} %broadcast_subtract_fusion.5, ...), kind=kLoop, calls=%fused_computation.59.clone.1 | loop fusion | flops 26208256 | bytes 100352 | tf_op jit(solution)/shard_map/while/body/eval_jaxpr/reduce_sum | solution.py:94
  474.9 19.4 %multiply_reduce_fusion.3 = (f32[4,512]{1,0:T(4,128)S(1)}, f32[4,512]{1,0:T(4,128)S(1)}, f32[4,512]{1,0:T(4,128)S(1)}) fusion(f32[512,4]{0,1:T(4,128)S(1)} %get-tuple-element.927, f32[512,4]{0,1:T(4,128)S(1)} %get-tuple-element.928, f32[512,4]{0,1:T(4,128)S(1)} %get-tuple-element.929, f32[4,512]{1,0:T(4,128)S(1)} %broadcast_subtract_fusion.5, ...), kind=kLoop, calls=%fused_computation.59.clone.1 | loop fusion | flops 26208256 | bytes 100352 | tf_op jit(solution)/shard_map/while/body/eval_jaxpr/reduce_sum | solution.py:94
  494.5 5.1 copy.33
  499.6 71.1 %reduce-scatter.4.cloned.1.call-done = f32[2048,3]{1,0:T(8,128)} async-done(((f32[16384,3]{1,0:T(8,128)}), f32[2048,3]{1,0:T(8,128)}) %reduce-scatter.4.cloned.1.call-update) | async-done | bytes 24592
  570.7 2.2 copy.34
  (350 shorter events, 49.2 us)
Async XLA Ops:
  7.9 78.3 %all-to-all-start = ((f32[8,1,2048]{2,1,0:T(1,128)}), f32[8,1,2048]{2,1,0:T(1,128)S(1)}, u32[]{:S(2)}, u32[]{:S(2)}) async-start(f32[8,1,2048]{2,1,0:T(1,128)} %stack.12), calls=%async_computation | async-start | bytes 131072 | tf_op jit(solution)/shard_map/all_to_all | solution.py:19
  14.3 556.4 %reduce-scatter.4.cloned.1.call-start = ((), (), s32[]{:S(2)}) async-start(), calls=%async_computation.2 | async-start | bytes 9437184
Sparse Core Ops, SparseCore 0:
  499.7 70.9 reduce-scatter.3
